TPU v7x, 512 devices: a whole 4x8x8 slice. The times are simulated.
512 devices in a mesh: space: 64 (over z_lo, x, y), tm: 8 (over z_hi, core).
Axes of the slice: x: 4, y: 8, z: 8 (z_hi: 4, z_lo: 2; z = z_hi * 2 + z_lo), core: 2. Of those that a mesh axis runs over, the one named last changes fastest.
Arguments:
- source: bfloat16 [16, 128, 4, 2, 3, 16, 128], P('tm', 'space'), may hold values from -6 to 6
- gauge_links: bfloat16 [16, 128, 4, 2, 3, 3, 128], P('tm', 'space'), may hold values from -2.5 to 2.5
- clover: bfloat16 [16, 128, 2, 2, 6, 6, 128], P('tm', 'space'), may hold values from -0.3984375 to 0.3984375
- eigenvectors: bfloat16 [16, 128, 2, 3, 256, 128], P('tm', 'space'), may hold values from -4 to 4
- elemental: bfloat16 [16, 2, 256, 256], P('tm'), may hold values from -0.25 to 0.25
Outputs:
- sink_field: bfloat16 [16, 128, 4, 2, 3, 16, 128], P('tm', 'space')
All inputs are finite; a program needn't handle non-finite values.
Results may differ from a plain program's by a relative error of at most 0.0057.
Values may be sent and summed in bfloat16 or wider, within the bound.
No kernel may reach another device: no remote copies, remote signals or barrier semaphores. Data moves between devices by JAX's collectives and lax.ppermute only.
A program may use at most 64 MiB of HBM per device.

v0:
```python
import jax
import jax.numpy as jnp
from jax import lax
from jax.sharding import PartitionSpec as P

X = 16
Y = 8
HOPPING = 0.125
HALF_MAP = (
    ((1, 0.0, -1.0), (0, 0.0, -1.0)),
    ((1, -1.0, 0.0), (0, 1.0, 0.0)),
    ((0, 0.0, -1.0), (1, 0.0, 1.0)),
    ((0, 1.0, 0.0), (1, 1.0, 0.0)),
)


def passed_along(value, axis, by):
    count = lax.axis_size(axis)
    return lax.ppermute(value, axis, [(i, (i + by) % count) for i in range(count)])


def extended(cells, sides, width):
    for axis, dim in sides:
        count = lax.axis_size(axis)
        head = lax.slice_in_dim(cells, 0, width, axis=dim)
        tail = lax.slice_in_dim(cells, cells.shape[dim] - width, cells.shape[dim], axis=dim)
        cells = jnp.concatenate(
            [
                lax.ppermute(tail, axis, [(i, (i + 1) % count) for i in range(count)]),
                cells,
                lax.ppermute(head, axis, [((i + 1) % count, i) for i in range(count)]),
            ],
            axis=dim,
        )
    return cells


def dagger_map(forward_map):
    result = [None, None]
    for row_number in range(2):
        column, real_coef, imag_coef = forward_map[row_number]
        result[column] = (row_number, real_coef, -imag_coef)
    return tuple(result)


def apply_half(spin_map, half_spinor):
    outputs = []
    for column, real_coef, imag_coef in spin_map:
        picked = half_spinor[:, :, column]
        real_in = picked[:, :, 0]
        imag_in = picked[:, :, 1]
        outputs.append(
            jnp.stack(
                [
                    real_coef * real_in - imag_coef * imag_in,
                    real_coef * imag_in + imag_coef * real_in,
                ],
                axis=2,
            )
        )
    return jnp.stack(outputs, axis=2)


def project(spinor, spin_map, sign_value):
    return spinor[:, :, 0:2] + sign_value * apply_half(spin_map, spinor[:, :, 2:4])


def colour_apply(matrix, spinor):
    real_out = 0.0
    imag_out = 0.0
    for colour in range(3):
        left_real = matrix[:, :, 0, :, colour][:, :, None, :, None, :]
        left_imag = matrix[:, :, 1, :, colour][:, :, None, :, None, :]
        right_real = spinor[:, :, :, 0, colour][:, :, :, None]
        right_imag = spinor[:, :, :, 1, colour][:, :, :, None]
        real_out = real_out + left_real * right_real - left_imag * right_imag
        imag_out = imag_out + left_real * right_imag + left_imag * right_real
    return jnp.stack([real_out, imag_out], axis=3)


def adjoint(matrix):
    return jnp.stack(
        [jnp.swapaxes(matrix[:, :, 0], 2, 3), -jnp.swapaxes(matrix[:, :, 1], 2, 3)], axis=2
    )


def clover_apply(clover, spinor):
    block_list = []
    for chiral in range(2):
        clover_block = clover[:, :, chiral]
        new_shape = clover_block.shape[:2] + (2, 3, 6, clover_block.shape[-1])
        rows_real = clover_block[:, :, 0].reshape(new_shape)
        rows_imag = clover_block[:, :, 1].reshape(new_shape)
        real_out = 0.0
        imag_out = 0.0
        for source_index in range(6):
            spin_in = 2 * chiral + source_index // 3
            colour_in = source_index % 3
            left_real = rows_real[:, :, :, :, source_index][:, :, :, :, None, :]
            left_imag = rows_imag[:, :, :, :, source_index][:, :, :, :, None, :]
            right_real = spinor[:, :, spin_in, 0, colour_in][:, :, None, None]
            right_imag = spinor[:, :, spin_in, 1, colour_in][:, :, None, None]
            real_out = real_out + left_real * right_real - left_imag * right_imag
            imag_out = imag_out + left_real * right_imag + left_imag * right_real
        block_list.append(jnp.stack([real_out, imag_out], axis=3))
    return jnp.concatenate(block_list, axis=2)


def roll_plane(array_in, offset, hop_direction):
    sites = array_in.shape[-1]
    period = X if hop_direction == 0 else Y
    stride = 1 if hop_direction == 0 else X
    position = jnp.arange(sites) // stride % period
    if offset < 0:
        at_edge = position == period - 1
        wrapped = jnp.roll(array_in, (period - 1) * stride, axis=-1)
        plain = jnp.roll(array_in, -stride, axis=-1)
    else:
        at_edge = position == 0
        wrapped = jnp.roll(array_in, -(period - 1) * stride, axis=-1)
        plain = jnp.roll(array_in, stride, axis=-1)
    return jnp.where(at_edge, wrapped, plain)


def dirac_region(padded, centre_links, back_z, back_t, clover):
    centre = padded[1:-1, 1:-1]
    hopping = 0.0
    for hop_direction in range(4):
        forward_map = HALF_MAP[hop_direction]
        backward_map = dagger_map(forward_map)
        here_links = centre_links[:, :, hop_direction]
        if hop_direction < 2:
            ahead = roll_plane(project(centre, forward_map, -1.0), -1, hop_direction)
            behind = roll_plane(
                colour_apply(adjoint(here_links), project(centre, forward_map, 1.0)),
                1,
                hop_direction,
            )
        else:
            if hop_direction == 2:
                ahead_full = padded[1:-1, 2:]
                behind_full = padded[1:-1, :-2]
                behind_links = back_z
            else:
                ahead_full = padded[2:, 1:-1]
                behind_full = padded[:-2, 1:-1]
                behind_links = back_t
            ahead = project(ahead_full, forward_map, -1.0)
            behind = colour_apply(adjoint(behind_links), project(behind_full, forward_map, 1.0))
        forward_part = colour_apply(here_links, ahead)
        hopping = hopping + jnp.concatenate(
            [forward_part + behind, apply_half(backward_map, behind - forward_part)], axis=2
        )
    return centre + clover_apply(clover, centre) - HOPPING * hopping


def reverse_time(padded, depth_rows, position, tm_count):
    slices = padded.shape[0]
    slice_ids = jnp.arange(slices)
    negate = jnp.logical_or(
        jnp.logical_and(slice_ids < depth_rows, position == 0),
        jnp.logical_and(slice_ids >= slices - depth_rows, position == tm_count - 1),
    )
    factor = jnp.where(negate, -1.0, 1.0).astype(jnp.float32)
    return padded * factor.reshape((slices,) + (1,) * (padded.ndim - 1))


def mix_coefficients(elemental, coefficients):
    slices = coefficients.shape[0]
    eigen_count = coefficients.shape[1]
    complex_pairs = coefficients.reshape(slices, eigen_count, -1, 2)
    elemental_f32 = elemental.astype(jnp.float32)

    def product(left_factor, right_factor):
        return jnp.einsum(
            "ogs,osq->ogq", left_factor, right_factor, precision=lax.Precision.HIGHEST
        )

    mixed_real = product(elemental_f32[:, 0], complex_pairs[..., 0]) - product(
        elemental_f32[:, 1], complex_pairs[..., 1]
    )
    mixed_imag = product(elemental_f32[:, 0], complex_pairs[..., 1]) + product(
        elemental_f32[:, 1], complex_pairs[..., 0]
    )
    return (
        jnp.stack([mixed_real, mixed_imag], axis=-1)
        .reshape(slices, eigen_count, -1)
        .astype(jnp.bfloat16)
    )


def on_device(source, gauge_links, clover, eigenvectors, elemental):
    slices = source.shape[0]
    layers = source.shape[1]
    column_list = source.shape[5]
    eigen_count = eigenvectors.shape[4]
    tm_position = lax.axis_index("tm")
    tm_count = lax.axis_size("tm")
    links_f32 = gauge_links.astype(jnp.float32)
    clover_f32 = clover.astype(jnp.float32)
    edge_z = passed_along(gauge_links[:, -1:, 2], "space", 1)
    edge_t = passed_along(gauge_links[-1:, :, 3], "tm", 1)
    back_z = jnp.concatenate([edge_z, gauge_links[:, :-1, 2]], axis=1).astype(jnp.float32)
    back_t = jnp.concatenate([edge_t, gauge_links[:-1, :, 3]], axis=0).astype(jnp.float32)

    def apply_once(spinor_in):
        padded = extended(spinor_in, (("space", 1), ("tm", 0)), 1)
        padded = reverse_time(padded, 1, tm_position, tm_count)
        return dirac_region(padded, links_f32, back_z, back_t, clover_f32)

    def apply_twice(spinor_in):
        return apply_once(apply_once(spinor_in))

    forward = apply_twice(source.astype(jnp.float32))
    rounded = forward.astype(jnp.bfloat16)
    normaliser = (3.0 * X * Y * layers * lax.axis_size("space")) ** (-0.5)
    products = 0.0
    for colour in range(3):
        products = products + lax.dot_general(
            eigenvectors[:, :, :, colour],
            rounded[:, :, :, :, colour],
            (((1, 4), (1, 5)), ((0,), (0,))),
            preferred_element_type=jnp.float32,
        )
    real_part = products[:, 0, :, :, 0] + products[:, 1, :, :, 1]
    imag_part = products[:, 0, :, :, 1] - products[:, 1, :, :, 0]
    partial_sums = (
        jnp.stack([real_part, imag_part], axis=-1).reshape(slices, eigen_count, 8 * column_list)
        * normaliser
    )
    share_sums = lax.psum_scatter(partial_sums, "space", scatter_dimension=2, tiled=True)
    mixed_coef = lax.all_gather(
        mix_coefficients(elemental, share_sums), "space", axis=2, tiled=True
    )
    complex_pairs = mixed_coef.reshape(slices, eigen_count, 4, column_list, 2)
    mixed_real = complex_pairs[..., 0]
    mixed_imag = complex_pairs[..., 1]
    first_row = jnp.stack([mixed_real, mixed_imag], axis=3)
    second_row = jnp.stack([-mixed_imag, mixed_real], axis=3)
    left_operand = jnp.stack([first_row, second_row], axis=1)
    colour_parts = [
        lax.dot_general(
            left_operand,
            eigenvectors[:, :, :, colour],
            (((1, 2), (2, 3)), ((0,), (0,))),
            preferred_element_type=jnp.float32,
        )
        for colour in range(3)
    ]
    expanded = jnp.moveaxis(jnp.stack(colour_parts, axis=3), 5, 1) * eigen_count ** (-0.5)
    return apply_twice(expanded).astype(jnp.bfloat16)


def solution(mesh):
    placed = (
        P("tm", "space", None, None, None, None, None),
        P("tm", "space", None, None, None, None, None),
        P("tm", "space", None, None, None, None, None),
        P("tm", "space", None, None, None, None),
        P("tm", None, None, None),
    )
    return jax.shard_map(
        on_device,
        mesh=mesh,
        in_specs=placed,
        out_specs=P("tm", "space", None, None, None, None, None),
        check_vma=False,
    )
```

profile of v0, /device:TPU:129, one launch (start us, length us, event | category | flops | bytes accessed | tf_op | source)
XLA Modules:
  0.0 963.1 jit_solution(2014216765966501170)
XLA Ops:
  6.5 1.1 copy_convert_fusion
  7.8 3.2 collective-permute-start
  11.0 7.8 collective-permute-start.1
  18.8 0.7 fusion.202
  19.6 7.0 collective-permute-start.5
  26.5 0.7 slice_bitcast_fusion.379
  27.3 0.6 copy.764
  27.9 1.9 collective-permute-start.4
  29.8 0.9 copy_convert_fusion.1
  31.5 0.6 broadcast_compare_fusion
  33.5 1.9 collective-permute-start.2
  35.4 2.4 collective-permute-start.3
  37.8 0.8 maximum_convert_fusion
  38.8 13.6 %collective-permute-done.2 = f32[1,4,4,2,3,16,128]{6,5,1,3,0,4,2:T(8,128)S(1)} collective-permute-done((f32[1,4,4,2,3,16,128]{6,5,1,3,0,4,2:T(8,128)S(1)}, f32[1,4,4,2,3,16,128]{6,5,1,3,0,4,2:T(8,128)S(1)}, u32[]{:S(2)}, u32[]{:S(2)}) %collective-permute-start.2) | collective-permute-done | bytes 786464 | tf_op jit(solution)/shard_map/ppermute | solution.py:29
  52.4 6.9 collective-permute-done.3
  67.2 1.9 collective-permute-start.6
  69.2 7.6 collective-permute-start.7
  76.7 4.4 collective-permute-done.6
  81.2 1.8 collective-permute-done.7
  83.0 1.3 fusion.193
  84.3 5.4 collective-permute-start.8
  89.7 2.1 collective-permute-start.9
  91.9 1.3 dynamic-slice
  93.8 1.5 fusion.192
  95.3 9.9 %collective-permute-done.8 = f32[1,4,4,2,3,16,128]{6,5,1,3,0,4,2:T(8,128)} collective-permute-done((f32[1,4,4,2,3,16,128]{6,5,1,3,0,4,2:T(8,128)}, f32[1,4,4,2,3,16,128]{6,5,1,3,0,4,2:T(8,128)}, u32[]{:S(2)}, u32[]{:S(2)}) %collective-permute-start.8) | collective-permute-done | bytes 786464 | tf_op jit(solution)/shard_map/ppermute | solution.py:29
  105.1 7.8 collective-permute-done.9
  113.0 1.8 maximum_multiply_fusion.1
  124.2 0.9 copy.796
  125.2 530.7 %all-reduce.3.cloned.1.call-done = f32[2,256,128]{1,0,2:T(2,128)} async-done(((f32[2,256,128]{1,0,2:T(2,128)}), f32[2,256,128]{1,0,2:T(2,128)}) %all-reduce.3.cloned.1.call-update) | async-done | bytes 262160
  655.9 0.7 dynamic-slice_bitcast_fusion
  657.9 125.5 %all-gather = bf16[2,256,1,128]{1,0,2,3:T(2,128)(2,1)S(1)} all-gather(bf16[2,256,1,2]{1,0,2,3:T(2,128)(2,1)S(1)} %pad_maximum_fusion.50), channel_id=2, replica_groups=mesh['space'=64,'tm'=8] {'space'}, dimensions={3}, use_global_device_ids=true | all-gather | bytes 133120 | tf_op jit(solution)/shard_map/all_gather | solution.py:232
  784.5 1.9 collective-permute-start.10
  786.4 7.6 collective-permute-start.11
  794.0 3.2 collective-permute-done.10
  797.2 1.5 collective-permute-done.11
  799.1 65.2 %collective-permute-start.12 = (f32[1,4,4,2,3,16,128]{6,5,1,3,0,4,2:T(8,128)S(1)}, f32[1,4,4,2,3,16,128]{6,5,1,3,0,4,2:T(8,128)S(1)}, u32[]{:S(2)}, u32[]{:S(2)}) collective-permute-start(f32[1,4,4,2,3,16,128]{6,5,1,3,0,4,2:T(8,128)S(1)} %get-tuple-element.180), channel_id=1, source_target_pairs={{0,1},{1,2},{2,3},{3,4},{4,5},{5,6},{6,7},{7,0},{8,9},{9,10},{10,1... | collective-permute-start | bytes 2359304 | tf_op jit(solution)/shard_map/ppermute | solution.py:29
  864.3 2.1 collective-permute-start.13
  866.4 15.2 %collective-permute-done.12 = f32[1,4,4,2,3,16,128]{6,5,1,3,0,4,2:T(8,128)S(1)} collective-permute-done((f32[1,4,4,2,3,16,128]{6,5,1,3,0,4,2:T(8,128)S(1)}, f32[1,4,4,2,3,16,128]{6,5,1,3,0,4,2:T(8,128)S(1)}, u32[]{:S(2)}, u32[]{:S(2)}) %collective-permute-start.12) | collective-permute-done | bytes 786464 | tf_op jit(solution)/shard_map/ppermute | solution.py:29
  881.6 6.5 collective-permute-done.13
  888.1 0.6 maximum_multiply_fusion.2
  897.3 1.9 collective-permute-start.14
  899.2 10.6 %collective-permute-start.15 = (f32[2,1,4,2,3,16,128]{6,5,1,3,2,0,4:T(8,128)S(1)}, f32[2,1,4,2,3,16,128]{6,5,1,3,2,0,4:T(8,128)S(1)}, u32[]{:S(2)}, u32[]{:S(2)}) collective-permute-start(f32[2,1,4,2,3,16,128]{6,5,1,3,2,0,4:T(8,128)S(1)} %get-tuple-element.212), channel_id=1, source_target_pairs={{8,0},{16,8},{24,16},{32,24},{40,32},{48,40},{56,48},{64,56},{72,6... | collective-permute-start | bytes 1179656 | tf_op jit(solution)/shard_map/ppermute | solution.py:31
  909.7 7.4 collective-permute-done.14
  917.5 7.5 collective-permute-start.16
  925.0 2.2 collective-permute-start.17
  927.2 10.9 %collective-permute-done.16 = f32[1,4,4,2,3,16,128]{6,5,1,3,2,0,4:T(8,128)S(1)} collective-permute-done((f32[1,4,4,2,3,16,128]{6,5,1,3,2,0,4:T(8,128)S(1)}, f32[1,4,4,2,3,16,128]{6,5,1,3,2,0,4:T(8,128)S(1)}, u32[]{:S(2)}, u32[]{:S(2)}) %collective-permute-start.16) | collective-permute-done | bytes 786464 | tf_op jit(solution)/shard_map/ppermute | solution.py:29
  938.1 9.4 collective-permute-done.17
  955.4 0.8 copy.863
  (620 shorter events, 35.4 us)
Async XLA Ops:
  6.5 25.7 %copy-start.103 = (bf16[2,2,2,2,6,6,128]{6,3,5,4,2,1,0:T(2,128)(2,1)S(1)}, bf16[2,2,2,2,6,6,128]{6,3,5,4,2,1,0:T(2,128)(2,1)}, u32[]{:S(2)}) copy-start(bf16[2,2,2,2,6,6,128]{6,3,5,4,2,1,0:T(2,128)(2,1)} %param.7) | copy-start | bytes 442372
  6.5 649.4 %all-reduce.3.cloned.1.call-start = ((), (), s32[]{:S(2)}) async-start(), calls=%async_computation | async-start | bytes 524288
  7.8 25.4 %collective-permute-start = (f32[2,1,4,2,3,16,128]{6,5,1,3,0,4,2:T(8,128)S(1)}, f32[2,1,4,2,3,16,128]{6,5,1,3,0,4,2:T(8,128)S(1)}, u32[]{:S(2)}, u32[]{:S(2)}) collective-permute-start(f32[2,1,4,2,3,16,128]{6,5,1,3,0,4,2:T(8,128)S(1)} %get-tuple-element.247), channel_id=1, source_target_pairs={{0,8},{8,16},{16,24},{24,32},{32,40},{40,48},{48,56},{56,64},{64,7... | collective-permute-start | bytes 1179656 | tf_op jit(solution)/shard_map/ppermute | solution.py:29
  11.0 22.2 %collective-permute-start.1 = (f32[2,1,4,2,3,16,128]{6,5,1,3,0,4,2:T(8,128)S(1)}, f32[2,1,4,2,3,16,128]{6,5,1,3,0,4,2:T(8,128)S(1)}, u32[]{:S(2)}, u32[]{:S(2)}) collective-permute-start(f32[2,1,4,2,3,16,128]{6,5,1,3,0,4,2:T(8,128)S(1)} %get-tuple-element.248), channel_id=1, source_target_pairs={{8,0},{16,8},{24,16},{32,24},{40,32},{48,40},{56,48},{64,56},{72,6... | collective-permute-start | bytes 1179656 | tf_op jit(solution)/shard_map/ppermute | solution.py:31
  19.6 13.6 %collective-permute-start.5 = (bf16[1,2,2,3,3,128]{5,1,4,3,2,0:T(2,128)(2,1)S(1)}, bf16[1,2,2,3,3,128]{5,1,4,3,2,0:T(2,128)(2,1)S(1)}, u32[]{:S(2)}, u32[]{:S(2)}) collective-permute-start(bf16[1,2,2,3,3,128]{5,1,4,3,2,0:T(2,128)(2,1)S(1)} %bitcast.1310), channel_id=1, source_target_pairs={{0,1},{1,2},{2,3},{3,4},{4,5},{5,6},{6,7},{7,0},{8,9},{9,10},{10,1... | collective-permute-start | bytes 27656 | tf_op jit(solution)/shard_map/ppermute | solution.py:19
  27.9 9.9 %collective-permute-start.4 = (bf16[2,1,2,3,3,128]{5,1,4,3,2,0:T(2,128)(2,1)}, bf16[2,1,2,3,3,128]{5,1,4,3,2,0:T(2,128)(2,1)}, u32[]{:S(2)}, u32[]{:S(2)}) collective-permute-start(bf16[2,1,2,3,3,128]{5,1,4,3,2,0:T(2,128)(2,1)} %copy.764), channel_id=1, source_target_pairs={{0,8},{8,16},{16,24},{24,32},{32,40},{40,48},{48,56},{56,64},{64,7... | collective-permute-start | bytes 27656 | tf_op jit(solution)/shard_map/ppermute | solution.py:19
  32.1 32.4 %copy-start.31 = (f32[2,2,3,128]{3,1,2,0:T(2,128)}, f32[2,2,3,128]{3,1,2,0:T(2,128)S(1)}, u32[]{:S(2)}) copy-start(f32[2,2,3,128]{3,1,2,0:T(2,128)S(1)} %get-tuple-element.761) | copy-start | bytes 18436
  32.1 32.4 %copy-start.34 = (f32[2,2,3,128]{3,1,2,0:T(2,128)}, f32[2,2,3,128]{3,1,2,0:T(2,128)S(1)}, u32[]{:S(2)}) copy-start(f32[2,2,3,128]{3,1,2,0:T(2,128)S(1)} %get-tuple-element.762) | copy-start | bytes 18436
  32.1 32.4 %copy-start.37 = (f32[2,2,3,128]{3,1,2,0:T(2,128)}, f32[2,2,3,128]{3,1,2,0:T(2,128)S(1)}, u32[]{:S(2)}) copy-start(f32[2,2,3,128]{3,1,2,0:T(2,128)S(1)} %get-tuple-element.763) | copy-start | bytes 18436
  32.1 32.4 %copy-start.40 = (f32[2,2,3,128]{3,1,2,0:T(2,128)}, f32[2,2,3,128]{3,1,2,0:T(2,128)S(1)}, u32[]{:S(2)}) copy-start(f32[2,2,3,128]{3,1,2,0:T(2,128)S(1)} %get-tuple-element.764) | copy-start | bytes 18436
  32.1 32.4 %copy-start.43 = (f32[2,2,3,128]{3,1,2,0:T(2,128)}, f32[2,2,3,128]{3,1,2,0:T(2,128)S(1)}, u32[]{:S(2)}) copy-start(f32[2,2,3,128]{3,1,2,0:T(2,128)S(1)} %get-tuple-element.765) | copy-start | bytes 18436
  32.1 32.4 %copy-start.46 = (f32[2,2,3,128]{3,1,2,0:T(2,128)}, f32[2,2,3,128]{3,1,2,0:T(2,128)S(1)}, u32[]{:S(2)}) copy-start(f32[2,2,3,128]{3,1,2,0:T(2,128)S(1)} %get-tuple-element.766) | copy-start | bytes 18436
  32.1 28.6 %copy-start.67 = (f32[2,2,3,128]{3,1,2,0:T(2,128)}, f32[2,2,3,128]{3,1,2,0:T(2,128)S(1)}, u32[]{:S(2)}) copy-start(f32[2,2,3,128]{3,1,2,0:T(2,128)S(1)} %get-tuple-element.767) | copy-start | bytes 18436
  32.2 28.6 %copy-start.70 = (f32[2,2,3,128]{3,1,2,0:T(2,128)}, f32[2,2,3,128]{3,1,2,0:T(2,128)S(1)}, u32[]{:S(2)}) copy-start(f32[2,2,3,128]{3,1,2,0:T(2,128)S(1)} %get-tuple-element.768) | copy-start | bytes 18436
  32.2 28.6 %copy-start.73 = (f32[2,2,3,128]{3,1,2,0:T(2,128)}, f32[2,2,3,128]{3,1,2,0:T(2,128)S(1)}, u32[]{:S(2)}) copy-start(f32[2,2,3,128]{3,1,2,0:T(2,128)S(1)} %get-tuple-element.769) | copy-start | bytes 18436
  32.2 28.6 %copy-start.76 = (f32[2,2,3,128]{3,1,2,0:T(2,128)}, f32[2,2,3,128]{3,1,2,0:T(2,128)S(1)}, u32[]{:S(2)}) copy-start(f32[2,2,3,128]{3,1,2,0:T(2,128)S(1)} %get-tuple-element.770) | copy-start | bytes 18436
  32.2 28.6 %copy-start.79 = (f32[2,2,3,128]{3,1,2,0:T(2,128)}, f32[2,2,3,128]{3,1,2,0:T(2,128)S(1)}, u32[]{:S(2)}) copy-start(f32[2,2,3,128]{3,1,2,0:T(2,128)S(1)} %get-tuple-element.771) | copy-start | bytes 18436
  32.2 28.6 %copy-start.82 = (f32[2,2,3,128]{3,1,2,0:T(2,128)}, f32[2,2,3,128]{3,1,2,0:T(2,128)S(1)}, u32[]{:S(2)}) copy-start(f32[2,2,3,128]{3,1,2,0:T(2,128)S(1)} %get-tuple-element.772) | copy-start | bytes 18436
  33.0 29.8 %copy-start.13 = (f32[2,2,3,128]{3,1,2,0:T(2,128)}, f32[2,2,3,128]{3,1,2,0:T(2,128)S(1)}, u32[]{:S(2)}) copy-start(f32[2,2,3,128]{3,1,2,0:T(2,128)S(1)} %get-tuple-element.717) | copy-start | bytes 18436
  33.0 29.8 %copy-start.16 = (f32[2,2,3,128]{3,1,2,0:T(2,128)}, f32[2,2,3,128]{3,1,2,0:T(2,128)S(1)}, u32[]{:S(2)}) copy-start(f32[2,2,3,128]{3,1,2,0:T(2,128)S(1)} %get-tuple-element.718) | copy-start | bytes 18436
  33.0 29.8 %copy-start.19 = (f32[2,2,3,128]{3,1,2,0:T(2,128)}, f32[2,2,3,128]{3,1,2,0:T(2,128)S(1)}, u32[]{:S(2)}) copy-start(f32[2,2,3,128]{3,1,2,0:T(2,128)S(1)} %get-tuple-element.719) | copy-start | bytes 18436
  33.0 29.8 %copy-start.22 = (f32[2,2,3,128]{3,1,2,0:T(2,128)}, f32[2,2,3,128]{3,1,2,0:T(2,128)S(1)}, u32[]{:S(2)}) copy-start(f32[2,2,3,128]{3,1,2,0:T(2,128)S(1)} %get-tuple-element.720) | copy-start | bytes 18436
  33.0 29.8 %copy-start.25 = (f32[2,2,3,128]{3,1,2,0:T(2,128)}, f32[2,2,3,128]{3,1,2,0:T(2,128)S(1)}, u32[]{:S(2)}) copy-start(f32[2,2,3,128]{3,1,2,0:T(2,128)S(1)} %get-tuple-element.721) | copy-start | bytes 18436
  33.0 29.8 %copy-start.28 = (f32[2,2,3,128]{3,1,2,0:T(2,128)}, f32[2,2,3,128]{3,1,2,0:T(2,128)S(1)}, u32[]{:S(2)}) copy-start(f32[2,2,3,128]{3,1,2,0:T(2,128)S(1)} %get-tuple-element.722) | copy-start | bytes 18436
  33.0 30.5 %copy-start.1 = (f32[2,2,3,128]{3,1,2,0:T(2,128)}, f32[2,2,3,128]{3,1,2,0:T(2,128)S(1)}, u32[]{:S(2)}) copy-start(f32[2,2,3,128]{3,1,2,0:T(2,128)S(1)} %get-tuple-element.795) | copy-start | bytes 18436
  33.1 30.5 %copy-start.4 = (f32[2,2,3,128]{3,1,2,0:T(2,128)}, f32[2,2,3,128]{3,1,2,0:T(2,128)S(1)}, u32[]{:S(2)}) copy-start(f32[2,2,3,128]{3,1,2,0:T(2,128)S(1)} %get-tuple-element.796) | copy-start | bytes 18436
  33.1 30.5 %copy-start.7 = (f32[2,2,3,128]{3,1,2,0:T(2,128)}, f32[2,2,3,128]{3,1,2,0:T(2,128)S(1)}, u32[]{:S(2)}) copy-start(f32[2,2,3,128]{3,1,2,0:T(2,128)S(1)} %get-tuple-element.797) | copy-start | bytes 18436
  33.1 30.5 %copy-start.10 = (f32[2,2,3,128]{3,1,2,0:T(2,128)}, f32[2,2,3,128]{3,1,2,0:T(2,128)S(1)}, u32[]{:S(2)}) copy-start(f32[2,2,3,128]{3,1,2,0:T(2,128)S(1)} %get-tuple-element.798) | copy-start | bytes 18436
  33.1 26.1 %copy-start.110 = (f32[4]{0:T(128)}, f32[4]{0:T(128)S(1)}, u32[]{:S(2)}) copy-start(f32[4]{0:T(128)S(1)} %or_select_fusion) | copy-start | bytes 52
  33.5 18.9 %collective-permute-start.2 = (f32[1,4,4,2,3,16,128]{6,5,1,3,0,4,2:T(8,128)S(1)}, f32[1,4,4,2,3,16,128]{6,5,1,3,0,4,2:T(8,128)S(1)}, u32[]{:S(2)}, u32[]{:S(2)}) collective-permute-start(f32[1,4,4,2,3,16,128]{6,5,1,3,0,4,2:T(8,128)S(1)} %get-tuple-element.187), channel_id=1, source_target_pairs={{0,1},{1,2},{2,3},{3,4},{4,5},{5,6},{6,7},{7,0},{8,9},{9,10},{10,1... | collective-permute-start | bytes 2359304 | tf_op jit(solution)/shard_map/ppermute | solution.py:29
  35.4 23.8 %collective-permute-start.3 = (f32[1,4,4,2,3,16,128]{6,5,1,3,0,4,2:T(8,128)S(1)}, f32[1,4,4,2,3,16,128]{6,5,1,3,0,4,2:T(8,128)S(1)}, u32[]{:S(2)}, u32[]{:S(2)}) collective-permute-start(f32[1,4,4,2,3,16,128]{6,5,1,3,0,4,2:T(8,128)S(1)} %get-tuple-element.188), channel_id=1, source_target_pairs={{1,0},{2,1},{3,2},{4,3},{5,4},{6,5},{7,6},{0,7},{9,8},{10,9},{11,1... | collective-permute-start | bytes 2359304 | tf_op jit(solution)/shard_map/ppermute | solution.py:31
  38.7 25.0 %copy-start.49 = (f32[2,2,3,128]{3,1,2,0:T(2,128)}, f32[2,2,3,128]{3,1,2,0:T(2,128)S(1)}, u32[]{:S(2)}) copy-start(f32[2,2,3,128]{3,1,2,0:T(2,128)S(1)} %get-tuple-element.758) | copy-start | bytes 18436
  38.7 25.0 %copy-start.52 = (f32[2,2,3,128]{3,1,2,0:T(2,128)}, f32[2,2,3,128]{3,1,2,0:T(2,128)S(1)}, u32[]{:S(2)}) copy-start(f32[2,2,3,128]{3,1,2,0:T(2,128)S(1)} %get-tuple-element.759) | copy-start | bytes 18436
  38.7 25.0 %copy-start.55 = (f32[2,2,3,128]{3,1,2,0:T(2,128)}, f32[2,2,3,128]{3,1,2,0:T(2,128)S(1)}, u32[]{:S(2)}) copy-start(f32[2,2,3,128]{3,1,2,0:T(2,128)S(1)} %get-tuple-element.760) | copy-start | bytes 18436
  67.2 14.0 %collective-permute-start.6 = (f32[2,1,4,2,3,16,128]{6,5,1,3,0,4,2:T(8,128)S(1)}, f32[2,1,4,2,3,16,128]{6,5,1,3,0,4,2:T(8,128)S(1)}, u32[]{:S(2)}, u32[]{:S(2)}) collective-permute-start(f32[2,1,4,2,3,16,128]{6,5,1,3,0,4,2:T(8,128)S(1)} %get-tuple-element.235), channel_id=1, source_target_pairs={{0,8},{8,16},{16,24},{24,32},{32,40},{40,48},{48,56},{56,64},{64,7... | collective-permute-start | bytes 1179656 | tf_op jit(solution)/shard_map/ppermute | solution.py:29
  69.2 13.8 %collective-permute-start.7 = (f32[2,1,4,2,3,16,128]{6,5,1,3,0,4,2:T(8,128)S(1)}, f32[2,1,4,2,3,16,128]{6,5,1,3,0,4,2:T(8,128)S(1)}, u32[]{:S(2)}, u32[]{:S(2)}) collective-permute-start(f32[2,1,4,2,3,16,128]{6,5,1,3,0,4,2:T(8,128)S(1)} %get-tuple-element.236), channel_id=1, source_target_pairs={{8,0},{16,8},{24,16},{32,24},{40,32},{48,40},{56,48},{64,56},{72,6... | collective-permute-start | bytes 1179656 | tf_op jit(solution)/shard_map/ppermute | solution.py:31
  84.3 20.8 %collective-permute-start.8 = (f32[1,4,4,2,3,16,128]{6,5,1,3,0,4,2:T(8,128)}, f32[1,4,4,2,3,16,128]{6,5,1,3,0,4,2:T(8,128)}, u32[]{:S(2)}, u32[]{:S(2)}) collective-permute-start(f32[1,4,4,2,3,16,128]{6,5,1,3,0,4,2:T(8,128)} %get-tuple-element.185), channel_id=1, source_target_pairs={{0,1},{1,2},{2,3},{3,4},{4,5},{5,6},{6,7},{7,0},{8,9},{9,10},{10,1... | collective-permute-start | bytes 2359304 | tf_op jit(solution)/shard_map/ppermute | solution.py:29
  89.7 23.2 %collective-permute-start.9 = (f32[1,4,4,2,3,16,128]{6,5,1,3,0,4,2:T(8,128)}, f32[1,4,4,2,3,16,128]{6,5,1,3,0,4,2:T(8,128)}, u32[]{:S(2)}, u32[]{:S(2)}) collective-permute-start(f32[1,4,4,2,3,16,128]{6,5,1,3,0,4,2:T(8,128)} %get-tuple-element.186), channel_id=1, source_target_pairs={{1,0},{2,1},{3,2},{4,3},{5,4},{6,5},{7,6},{0,7},{9,8},{10,9},{11,1... | collective-permute-start | bytes 2359304 | tf_op jit(solution)/shard_map/ppermute | solution.py:31
  123.8 532.8 %copy-start = (bf16[2,2,256,256]{3,2,1,0:T(8,128)(2,1)S(1)}, bf16[2,2,256,256]{3,2,1,0:T(8,128)(2,1)}, u32[]{:S(2)}) copy-start(bf16[2,2,256,256]{3,2,1,0:T(8,128)(2,1)} %param.9) | copy-start | bytes 1572868
  784.5 12.7 %collective-permute-start.10 = (f32[2,1,4,2,3,16,128]{6,5,1,3,0,4,2:T(8,128)S(1)}, f32[2,1,4,2,3,16,128]{6,5,1,3,0,4,2:T(8,128)S(1)}, u32[]{:S(2)}, u32[]{:S(2)}) collective-permute-start(f32[2,1,4,2,3,16,128]{6,5,1,3,0,4,2:T(8,128)S(1)} %get-tuple-element.223), channel_id=1, source_target_pairs={{0,8},{8,16},{16,24},{24,32},{32,40},{40,48},{48,56},{56,64},{64,7... | collective-permute-start | bytes 1179656 | tf_op jit(solution)/shard_map/ppermute | solution.py:29
  786.4 101.7 %copy-start.111 = (f32[4]{0:T(128)S(1)}, f32[4]{0:T(128)}, u32[]{:S(2)}) copy-start(f32[4]{0:T(128)} %copy-done.110) | copy-start | bytes 52
  786.4 12.3 %collective-permute-start.11 = (f32[2,1,4,2,3,16,128]{6,5,1,3,0,4,2:T(8,128)S(1)}, f32[2,1,4,2,3,16,128]{6,5,1,3,0,4,2:T(8,128)S(1)}, u32[]{:S(2)}, u32[]{:S(2)}) collective-permute-start(f32[2,1,4,2,3,16,128]{6,5,1,3,0,4,2:T(8,128)S(1)} %get-tuple-element.224), channel_id=1, source_target_pairs={{8,0},{16,8},{24,16},{32,24},{40,32},{48,40},{56,48},{64,56},{72,6... | collective-permute-start | bytes 1179656 | tf_op jit(solution)/shard_map/ppermute | solution.py:31
  799.1 82.5 %collective-permute-start.12 = (f32[1,4,4,2,3,16,128]{6,5,1,3,0,4,2:T(8,128)S(1)}, f32[1,4,4,2,3,16,128]{6,5,1,3,0,4,2:T(8,128)S(1)}, u32[]{:S(2)}, u32[]{:S(2)}) collective-permute-start(f32[1,4,4,2,3,16,128]{6,5,1,3,0,4,2:T(8,128)S(1)} %get-tuple-element.180), channel_id=1, source_target_pairs={{0,1},{1,2},{2,3},{3,4},{4,5},{5,6},{6,7},{7,0},{8,9},{9,10},{10,1... | collective-permute-start | bytes 2359304 | tf_op jit(solution)/shard_map/ppermute | solution.py:29
  864.3 23.8 %collective-permute-start.13 = (f32[1,4,4,2,3,16,128]{6,5,1,3,0,4,2:T(8,128)S(1)}, f32[1,4,4,2,3,16,128]{6,5,1,3,0,4,2:T(8,128)S(1)}, u32[]{:S(2)}, u32[]{:S(2)}) collective-permute-start(f32[1,4,4,2,3,16,128]{6,5,1,3,0,4,2:T(8,128)S(1)} %get-tuple-element.181), channel_id=1, source_target_pairs={{1,0},{2,1},{3,2},{4,3},{5,4},{6,5},{7,6},{0,7},{9,8},{10,9},{11,1... | collective-permute-start | bytes 2359304 | tf_op jit(solution)/shard_map/ppermute | solution.py:31
  897.3 19.9 %collective-permute-start.14 = (f32[2,1,4,2,3,16,128]{6,5,1,3,2,0,4:T(8,128)S(1)}, f32[2,1,4,2,3,16,128]{6,5,1,3,2,0,4:T(8,128)S(1)}, u32[]{:S(2)}, u32[]{:S(2)}) collective-permute-start(f32[2,1,4,2,3,16,128]{6,5,1,3,2,0,4:T(8,128)S(1)} %get-tuple-element.211), channel_id=1, source_target_pairs={{0,8},{8,16},{16,24},{24,32},{32,40},{40,48},{48,56},{56,64},{64,7... | collective-permute-start | bytes 1179656 | tf_op jit(solution)/shard_map/ppermute | solution.py:29
  899.2 18.0 %collective-permute-start.15 = (f32[2,1,4,2,3,16,128]{6,5,1,3,2,0,4:T(8,128)S(1)}, f32[2,1,4,2,3,16,128]{6,5,1,3,2,0,4:T(8,128)S(1)}, u32[]{:S(2)}, u32[]{:S(2)}) collective-permute-start(f32[2,1,4,2,3,16,128]{6,5,1,3,2,0,4:T(8,128)S(1)} %get-tuple-element.212), channel_id=1, source_target_pairs={{8,0},{16,8},{24,16},{32,24},{40,32},{48,40},{56,48},{64,56},{72,6... | collective-permute-start | bytes 1179656 | tf_op jit(solution)/shard_map/ppermute | solution.py:31
  917.5 20.6 %collective-permute-start.16 = (f32[1,4,4,2,3,16,128]{6,5,1,3,2,0,4:T(8,128)S(1)}, f32[1,4,4,2,3,16,128]{6,5,1,3,2,0,4:T(8,128)S(1)}, u32[]{:S(2)}, u32[]{:S(2)}) collective-permute-start(f32[1,4,4,2,3,16,128]{6,5,1,3,2,0,4:T(8,128)S(1)} %get-tuple-element.178), channel_id=1, source_target_pairs={{0,1},{1,2},{2,3},{3,4},{4,5},{5,6},{6,7},{7,0},{8,9},{9,10},{10,1... | collective-permute-start | bytes 2359304 | tf_op jit(solution)/shard_map/ppermute | solution.py:29
  925.0 22.6 %collective-permute-start.17 = (f32[1,4,4,2,3,16,128]{6,5,1,3,2,0,4:T(8,128)S(1)}, f32[1,4,4,2,3,16,128]{6,5,1,3,2,0,4:T(8,128)S(1)}, u32[]{:S(2)}, u32[]{:S(2)}) collective-permute-start(f32[1,4,4,2,3,16,128]{6,5,1,3,2,0,4:T(8,128)S(1)} %get-tuple-element.179), channel_id=1, source_target_pairs={{1,0},{2,1},{3,2},{4,3},{5,4},{6,5},{7,6},{0,7},{9,8},{10,9},{11,1... | collective-permute-start | bytes 2359304 | tf_op jit(solution)/shard_map/ppermute | solution.py:31
  (83 other events, 286.6 us)
Sparse Core Ops, SparseCore 0:
  125.2 530.6 all-reduce.2
where the time goes:
time: 964 us; the launch traced here: 963 us
  waiting for transfers between devices  629 us (65%)
  starting transfers between devices  140 us (15%)
  blocking collectives  125 us (13%)
  other arithmetic  30.5 us (3%)
  between operations  18.4 us (2%)
  local copies, waits for them, and re-layouts  16.3 us (2%)
    unnamed x2, waiting for transfers between devices  531 us
    all_gather x1, blocking collectives, on_device(): lax.all_gather(mix_coefficients(elemental, share_sums), 'space', axis=2,...  125 us
    ppermute x8, starting transfers between devices, extended(): lax.ppermute(tail, axis, [(i, (i + 1) % count) for i in range(count)])  89 us
    ppermute x8, waiting for transfers between devices, extended(): lax.ppermute(tail, axis, [(i, (i + 1) % count) for i in range(count)])  64.6 us
    ppermute x8, starting transfers between devices, extended(): lax.ppermute(head, axis, [((i + 1) % count, i) for i in range(count)])  42.4 us
    ppermute x8, waiting for transfers between devices, extended(): lax.ppermute(head, axis, [((i + 1) % count, i) for i in range(count)])  34 us
  transfers between devices with their start and end apart: 19, of which 14 were waited for; matrix products, arithmetic and copies ran while one was open for 1% of the time, Pallas kernels for 0%

commit v1 on v0

--- a/solution.py
+++ b/solution.py
@@ -229,9 +229,9 @@
         * normaliser
     )
     share_sums = lax.psum_scatter(partial_sums, "space", scatter_dimension=2, tiled=True)
-    mixed_coef = lax.all_gather(
-        mix_coefficients(elemental, share_sums), "space", axis=2, tiled=True
-    )
+    part = mix_coefficients(elemental, share_sums)
+    sent = jnp.stack([part] * lax.axis_size("space"))
+    mixed_coef = jnp.concatenate(lax.all_to_all(sent, "space", 0, 0), axis=2)
     complex_pairs = mixed_coef.reshape(slices, eigen_count, 4, column_list, 2)
     mixed_real = complex_pairs[..., 0]
     mixed_imag = complex_pairs[..., 1]

time: 964 us -> 819 us (0.85)
  the two profiles are of different devices: /device:TPU:129 before, /device:TPU:191 now
where the time goes in v1:
time: 819 us; the launch traced here: 818 us
  waiting for transfers between devices  649 us (79%)
  starting transfers between devices  107 us (13%)
  other arithmetic  27.8 us (3%)
  between operations  18 us (2%)
  local copies, waits for them, and re-layouts  13.2 us (2%)
    unnamed x2, waiting for transfers between devices  528 us
    ppermute x8, waiting for transfers between devices, extended(): lax.ppermute(tail, axis, [(i, (i + 1) % count) for i in range(count)])  68.8 us
    ppermute x8, starting transfers between devices, extended(): lax.ppermute(tail, axis, [(i, (i + 1) % count) for i in range(count)])  65.2 us
    ppermute x8, waiting for transfers between devices, extended(): lax.ppermute(head, axis, [((i + 1) % count, i) for i in range(count)])  45.8 us
    ppermute x8, starting transfers between devices, extended(): lax.ppermute(head, axis, [((i + 1) % count, i) for i in range(count)])  19.3 us
  transfers between devices with their start and end apart: 20, of which 16 were waited for; matrix products, arithmetic and copies ran while one was open for 1% of the time, Pallas kernels for 0%

profile of v1, /device:TPU:191, one launch (start us, length us, event | category | flops | bytes accessed | tf_op | source)
XLA Modules:
  0.0 818.2 jit_solution(7010871602118955236)
XLA Ops:
  6.5 1.1 copy_convert_fusion
  7.8 3.1 collective-permute-start
  10.9 2.2 collective-permute-start.1
  13.1 0.7 fusion.201
  13.8 8.1 collective-permute-start.5
  22.0 0.7 slice_bitcast_fusion.381
  22.8 6.4 collective-permute-start.4
  29.2 0.9 copy_convert_fusion.1
  31.8 3.0 collective-permute-start.2
  34.8 1.9 collective-permute-start.3
  37.0 15.0 %collective-permute-done.2 = f32[1,4,4,2,3,16,128]{6,5,1,3,0,4,2:T(8,128)S(1)} collective-permute-done((f32[1,4,4,2,3,16,128]{6,5,1,3,0,4,2:T(8,128)S(1)}, f32[1,4,4,2,3,16,128]{6,5,1,3,0,4,2:T(8,128)S(1)}, u32[]{:S(2)}, u32[]{:S(2)}) %collective-permute-start.2) | collective-permute-done | bytes 786464 | tf_op jit(solution)/shard_map/ppermute | solution.py:29
  52.0 6.3 collective-permute-done.3
  58.3 0.6 maximum_multiply_fusion
  66.2 1.9 collective-permute-start.6
  68.2 3.5 collective-permute-start.7
  71.7 3.9 collective-permute-done.6
  75.5 6.0 collective-permute-done.7
  81.8 5.7 collective-permute-start.8
  87.5 2.1 collective-permute-start.9
  89.8 15.0 %collective-permute-done.8 = f32[1,4,4,2,3,16,128]{6,5,1,3,0,4,2:T(8,128)S(1)} collective-permute-done((f32[1,4,4,2,3,16,128]{6,5,1,3,0,4,2:T(8,128)S(1)}, f32[1,4,4,2,3,16,128]{6,5,1,3,0,4,2:T(8,128)S(1)}, u32[]{:S(2)}, u32[]{:S(2)}) %collective-permute-start.8) | collective-permute-done | bytes 786464 | tf_op jit(solution)/shard_map/ppermute | solution.py:29
  104.8 4.9 collective-permute-done.9
  109.7 0.6 maximum_multiply_fusion.1
  119.0 0.9 copy.792
  119.9 1.3 dynamic-slice
  121.8 528.1 %all-reduce.3.cloned.1.call-done = f32[2,256,128]{1,0,2:T(2,128)} async-done(((f32[2,256,128]{1,0,2:T(2,128)}), f32[2,256,128]{1,0,2:T(2,128)}) %all-reduce.3.cloned.1.call-update) | async-done | bytes 262160
  649.9 0.7 dynamic-slice_bitcast_fusion
  651.9 0.7 stack.619
  652.6 8.0 all-to-all-start
  660.7 6.5 all-to-all-done
  668.2 6.2 collective-permute-start.10
  674.5 1.9 collective-permute-start.11
  676.4 2.8 collective-permute-done.10
  679.1 8.1 collective-permute-done.11
  687.5 37.1 %collective-permute-start.12 = (f32[1,4,4,2,3,16,128]{6,5,1,3,0,4,2:T(8,128)S(1)}, f32[1,4,4,2,3,16,128]{6,5,1,3,0,4,2:T(8,128)S(1)}, u32[]{:S(2)}, u32[]{:S(2)}) collective-permute-start(f32[1,4,4,2,3,16,128]{6,5,1,3,0,4,2:T(8,128)S(1)} %get-tuple-element.180), channel_id=1, source_target_pairs={{0,1},{1,2},{2,3},{3,4},{4,5},{5,6},{6,7},{7,0},{8,9},{9,10},{10,1... | collective-permute-start | bytes 2359304 | tf_op jit(solution)/shard_map/ppermute | solution.py:29
  724.7 2.1 collective-permute-start.13
  726.8 13.9 %collective-permute-done.12 = f32[1,4,4,2,3,16,128]{6,5,1,3,0,4,2:T(8,128)S(1)} collective-permute-done((f32[1,4,4,2,3,16,128]{6,5,1,3,0,4,2:T(8,128)S(1)}, f32[1,4,4,2,3,16,128]{6,5,1,3,0,4,2:T(8,128)S(1)}, u32[]{:S(2)}, u32[]{:S(2)}) %collective-permute-start.12) | collective-permute-done | bytes 786464 | tf_op jit(solution)/shard_map/ppermute | solution.py:29
  740.7 7.8 collective-permute-done.13
  748.5 0.6 maximum_multiply_fusion.2
  757.0 0.6 fusion.12
  757.6 1.9 collective-permute-start.14
  759.6 3.4 collective-permute-start.15
  762.9 3.5 collective-permute-done.14
  766.4 5.9 collective-permute-done.15
  772.6 6.2 collective-permute-start.16
  778.9 2.2 collective-permute-start.17
  781.1 14.8 %collective-permute-done.16 = f32[1,4,4,2,3,16,128]{6,5,1,3,2,0,4:T(8,128)S(1)} collective-permute-done((f32[1,4,4,2,3,16,128]{6,5,1,3,2,0,4:T(8,128)S(1)}, f32[1,4,4,2,3,16,128]{6,5,1,3,2,0,4:T(8,128)S(1)}, u32[]{:S(2)}, u32[]{:S(2)}) %collective-permute-start.16) | collective-permute-done | bytes 786464 | tf_op jit(solution)/shard_map/ppermute | solution.py:29
  795.8 6.8 collective-permute-done.17
  810.5 0.8 copy.858
  (551 shorter events, 33.5 us)
Async XLA Ops:
  6.5 643.4 %all-reduce.3.cloned.1.call-start = ((), (), s32[]{:S(2)}) async-start(), calls=%async_computation.1 | async-start | bytes 524288
  7.8 23.7 %collective-permute-start = (f32[2,1,4,2,3,16,128]{6,5,1,3,0,4,2:T(8,128)S(1)}, f32[2,1,4,2,3,16,128]{6,5,1,3,0,4,2:T(8,128)S(1)}, u32[]{:S(2)}, u32[]{:S(2)}) collective-permute-start(f32[2,1,4,2,3,16,128]{6,5,1,3,0,4,2:T(8,128)S(1)} %get-tuple-element.247), channel_id=1, source_target_pairs={{0,8},{8,16},{16,24},{24,32},{32,40},{40,48},{48,56},{56,64},{64,7... | collective-permute-start | bytes 1179656 | tf_op jit(solution)/shard_map/ppermute | solution.py:29
  10.9 20.6 %collective-permute-start.1 = (f32[2,1,4,2,3,16,128]{6,5,1,3,0,4,2:T(8,128)S(1)}, f32[2,1,4,2,3,16,128]{6,5,1,3,0,4,2:T(8,128)S(1)}, u32[]{:S(2)}, u32[]{:S(2)}) collective-permute-start(f32[2,1,4,2,3,16,128]{6,5,1,3,0,4,2:T(8,128)S(1)} %get-tuple-element.248), channel_id=1, source_target_pairs={{8,0},{16,8},{24,16},{32,24},{40,32},{48,40},{56,48},{64,56},{72,6... | collective-permute-start | bytes 1179656 | tf_op jit(solution)/shard_map/ppermute | solution.py:31
  13.8 17.6 %collective-permute-start.5 = (bf16[1,2,2,3,3,128]{5,1,4,3,2,0:T(2,128)(2,1)S(1)}, bf16[1,2,2,3,3,128]{5,1,4,3,2,0:T(2,128)(2,1)S(1)}, u32[]{:S(2)}, u32[]{:S(2)}) collective-permute-start(bf16[1,2,2,3,3,128]{5,1,4,3,2,0:T(2,128)(2,1)S(1)} %bitcast.1311), channel_id=1, source_target_pairs={{0,1},{1,2},{2,3},{3,4},{4,5},{5,6},{6,7},{7,0},{8,9},{9,10},{10,1... | collective-permute-start | bytes 27656 | tf_op jit(solution)/shard_map/ppermute | solution.py:19
  22.8 14.0 %collective-permute-start.4 = (bf16[2,1,2,3,3,128]{5,1,4,3,2,0:T(2,128)(2,1)S(1)}, bf16[2,1,2,3,3,128]{5,1,4,3,2,0:T(2,128)(2,1)S(1)}, u32[]{:S(2)}, u32[]{:S(2)}) collective-permute-start(bf16[2,1,2,3,3,128]{5,1,4,3,2,0:T(2,128)(2,1)S(1)} %copy.760), channel_id=1, source_target_pairs={{0,8},{8,16},{16,24},{24,32},{32,40},{40,48},{48,56},{56,64},{64,7... | collective-permute-start | bytes 27656 | tf_op jit(solution)/shard_map/ppermute | solution.py:19
  30.3 86.0 %copy-start.73 = (pred[128]{0:T(512)(128)(4,1)}, pred[128]{0:T(512)(128)(4,1)S(1)}, u32[]{:S(2)}) copy-start(pred[128]{0:T(512)(128)(4,1)S(1)} %broadcast_compare_fusion.1) | copy-start | bytes 388
  30.3 86.5 %copy-start.71 = (pred[128]{0:T(512)(128)(4,1)}, pred[128]{0:T(512)(128)(4,1)S(1)}, u32[]{:S(2)}) copy-start(pred[128]{0:T(512)(128)(4,1)S(1)} %broadcast_compare_fusion) | copy-start | bytes 388
  30.3 84.9 %copy-start.22 = (f32[2,2,3,128]{3,1,2,0:T(2,128)}, f32[2,2,3,128]{3,1,2,0:T(2,128)S(1)}, u32[]{:S(2)}) copy-start(f32[2,2,3,128]{3,1,2,0:T(2,128)S(1)} %get-tuple-element.761) | copy-start | bytes 18436
  30.3 84.9 %copy-start.24 = (f32[2,2,3,128]{3,1,2,0:T(2,128)}, f32[2,2,3,128]{3,1,2,0:T(2,128)S(1)}, u32[]{:S(2)}) copy-start(f32[2,2,3,128]{3,1,2,0:T(2,128)S(1)} %get-tuple-element.762) | copy-start | bytes 18436
  30.4 84.9 %copy-start.26 = (f32[2,2,3,128]{3,1,2,0:T(2,128)}, f32[2,2,3,128]{3,1,2,0:T(2,128)S(1)}, u32[]{:S(2)}) copy-start(f32[2,2,3,128]{3,1,2,0:T(2,128)S(1)} %get-tuple-element.763) | copy-start | bytes 18436
  30.4 84.9 %copy-start.28 = (f32[2,2,3,128]{3,1,2,0:T(2,128)}, f32[2,2,3,128]{3,1,2,0:T(2,128)S(1)}, u32[]{:S(2)}) copy-start(f32[2,2,3,128]{3,1,2,0:T(2,128)S(1)} %get-tuple-element.764) | copy-start | bytes 18436
  30.4 84.9 %copy-start.30 = (f32[2,2,3,128]{3,1,2,0:T(2,128)}, f32[2,2,3,128]{3,1,2,0:T(2,128)S(1)}, u32[]{:S(2)}) copy-start(f32[2,2,3,128]{3,1,2,0:T(2,128)S(1)} %get-tuple-element.765) | copy-start | bytes 18436
  30.4 84.9 %copy-start.32 = (f32[2,2,3,128]{3,1,2,0:T(2,128)}, f32[2,2,3,128]{3,1,2,0:T(2,128)S(1)}, u32[]{:S(2)}) copy-start(f32[2,2,3,128]{3,1,2,0:T(2,128)S(1)} %get-tuple-element.766) | copy-start | bytes 18436
  30.4 82.1 %copy-start.46 = (f32[2,2,3,128]{3,1,2,0:T(2,128)}, f32[2,2,3,128]{3,1,2,0:T(2,128)S(1)}, u32[]{:S(2)}) copy-start(f32[2,2,3,128]{3,1,2,0:T(2,128)S(1)} %get-tuple-element.767) | copy-start | bytes 18436
  30.4 82.1 %copy-start.48 = (f32[2,2,3,128]{3,1,2,0:T(2,128)}, f32[2,2,3,128]{3,1,2,0:T(2,128)S(1)}, u32[]{:S(2)}) copy-start(f32[2,2,3,128]{3,1,2,0:T(2,128)S(1)} %get-tuple-element.768) | copy-start | bytes 18436
  30.4 82.1 %copy-start.50 = (f32[2,2,3,128]{3,1,2,0:T(2,128)}, f32[2,2,3,128]{3,1,2,0:T(2,128)S(1)}, u32[]{:S(2)}) copy-start(f32[2,2,3,128]{3,1,2,0:T(2,128)S(1)} %get-tuple-element.769) | copy-start | bytes 18436
  30.5 82.1 %copy-start.52 = (f32[2,2,3,128]{3,1,2,0:T(2,128)}, f32[2,2,3,128]{3,1,2,0:T(2,128)S(1)}, u32[]{:S(2)}) copy-start(f32[2,2,3,128]{3,1,2,0:T(2,128)S(1)} %get-tuple-element.770) | copy-start | bytes 18436
  30.5 82.1 %copy-start.54 = (f32[2,2,3,128]{3,1,2,0:T(2,128)}, f32[2,2,3,128]{3,1,2,0:T(2,128)S(1)}, u32[]{:S(2)}) copy-start(f32[2,2,3,128]{3,1,2,0:T(2,128)S(1)} %get-tuple-element.771) | copy-start | bytes 18436
  30.5 82.1 %copy-start.56 = (f32[2,2,3,128]{3,1,2,0:T(2,128)}, f32[2,2,3,128]{3,1,2,0:T(2,128)S(1)}, u32[]{:S(2)}) copy-start(f32[2,2,3,128]{3,1,2,0:T(2,128)S(1)} %get-tuple-element.772) | copy-start | bytes 18436
  31.3 82.3 %copy-start.10 = (f32[2,2,3,128]{3,1,2,0:T(2,128)}, f32[2,2,3,128]{3,1,2,0:T(2,128)S(1)}, u32[]{:S(2)}) copy-start(f32[2,2,3,128]{3,1,2,0:T(2,128)S(1)} %get-tuple-element.717) | copy-start | bytes 18436
  31.3 82.3 %copy-start.12 = (f32[2,2,3,128]{3,1,2,0:T(2,128)}, f32[2,2,3,128]{3,1,2,0:T(2,128)S(1)}, u32[]{:S(2)}) copy-start(f32[2,2,3,128]{3,1,2,0:T(2,128)S(1)} %get-tuple-element.718) | copy-start | bytes 18436
  31.3 82.3 %copy-start.14 = (f32[2,2,3,128]{3,1,2,0:T(2,128)}, f32[2,2,3,128]{3,1,2,0:T(2,128)S(1)}, u32[]{:S(2)}) copy-start(f32[2,2,3,128]{3,1,2,0:T(2,128)S(1)} %get-tuple-element.719) | copy-start | bytes 18436
  31.3 82.3 %copy-start.16 = (f32[2,2,3,128]{3,1,2,0:T(2,128)}, f32[2,2,3,128]{3,1,2,0:T(2,128)S(1)}, u32[]{:S(2)}) copy-start(f32[2,2,3,128]{3,1,2,0:T(2,128)S(1)} %get-tuple-element.720) | copy-start | bytes 18436
  31.3 82.3 %copy-start.18 = (f32[2,2,3,128]{3,1,2,0:T(2,128)}, f32[2,2,3,128]{3,1,2,0:T(2,128)S(1)}, u32[]{:S(2)}) copy-start(f32[2,2,3,128]{3,1,2,0:T(2,128)S(1)} %get-tuple-element.721) | copy-start | bytes 18436
  31.3 82.3 %copy-start.20 = (f32[2,2,3,128]{3,1,2,0:T(2,128)}, f32[2,2,3,128]{3,1,2,0:T(2,128)S(1)}, u32[]{:S(2)}) copy-start(f32[2,2,3,128]{3,1,2,0:T(2,128)S(1)} %get-tuple-element.722) | copy-start | bytes 18436
  31.3 82.9 %copy-start.2 = (f32[2,2,3,128]{3,1,2,0:T(2,128)}, f32[2,2,3,128]{3,1,2,0:T(2,128)S(1)}, u32[]{:S(2)}) copy-start(f32[2,2,3,128]{3,1,2,0:T(2,128)S(1)} %get-tuple-element.795) | copy-start | bytes 18436
  31.3 82.9 %copy-start.4 = (f32[2,2,3,128]{3,1,2,0:T(2,128)}, f32[2,2,3,128]{3,1,2,0:T(2,128)S(1)}, u32[]{:S(2)}) copy-start(f32[2,2,3,128]{3,1,2,0:T(2,128)S(1)} %get-tuple-element.796) | copy-start | bytes 18436
  31.4 82.9 %copy-start.6 = (f32[2,2,3,128]{3,1,2,0:T(2,128)}, f32[2,2,3,128]{3,1,2,0:T(2,128)S(1)}, u32[]{:S(2)}) copy-start(f32[2,2,3,128]{3,1,2,0:T(2,128)S(1)} %get-tuple-element.797) | copy-start | bytes 18436
  31.4 82.9 %copy-start.8 = (f32[2,2,3,128]{3,1,2,0:T(2,128)}, f32[2,2,3,128]{3,1,2,0:T(2,128)S(1)}, u32[]{:S(2)}) copy-start(f32[2,2,3,128]{3,1,2,0:T(2,128)S(1)} %get-tuple-element.798) | copy-start | bytes 18436
  31.4 78.3 %copy-start.75 = (f32[4]{0:T(128)}, f32[4]{0:T(128)S(1)}, u32[]{:S(2)}) copy-start(f32[4]{0:T(128)S(1)} %or_select_fusion) | copy-start | bytes 52
  31.8 20.2 %collective-permute-start.2 = (f32[1,4,4,2,3,16,128]{6,5,1,3,0,4,2:T(8,128)S(1)}, f32[1,4,4,2,3,16,128]{6,5,1,3,0,4,2:T(8,128)S(1)}, u32[]{:S(2)}, u32[]{:S(2)}) collective-permute-start(f32[1,4,4,2,3,16,128]{6,5,1,3,0,4,2:T(8,128)S(1)} %get-tuple-element.187), channel_id=1, source_target_pairs={{0,1},{1,2},{2,3},{3,4},{4,5},{5,6},{6,7},{7,0},{8,9},{9,10},{10,1... | collective-permute-start | bytes 2359304 | tf_op jit(solution)/shard_map/ppermute | solution.py:29
  34.8 23.5 %collective-permute-start.3 = (f32[1,4,4,2,3,16,128]{6,5,1,3,0,4,2:T(8,128)S(1)}, f32[1,4,4,2,3,16,128]{6,5,1,3,0,4,2:T(8,128)S(1)}, u32[]{:S(2)}, u32[]{:S(2)}) collective-permute-start(f32[1,4,4,2,3,16,128]{6,5,1,3,0,4,2:T(8,128)S(1)} %get-tuple-element.188), channel_id=1, source_target_pairs={{1,0},{2,1},{3,2},{4,3},{5,4},{6,5},{7,6},{0,7},{9,8},{10,9},{11,1... | collective-permute-start | bytes 2359304 | tf_op jit(solution)/shard_map/ppermute | solution.py:31
  36.9 77.6 %copy-start.34 = (f32[2,2,3,128]{3,1,2,0:T(2,128)}, f32[2,2,3,128]{3,1,2,0:T(2,128)S(1)}, u32[]{:S(2)}) copy-start(f32[2,2,3,128]{3,1,2,0:T(2,128)S(1)} %get-tuple-element.758) | copy-start | bytes 18436
  36.9 77.6 %copy-start.36 = (f32[2,2,3,128]{3,1,2,0:T(2,128)}, f32[2,2,3,128]{3,1,2,0:T(2,128)S(1)}, u32[]{:S(2)}) copy-start(f32[2,2,3,128]{3,1,2,0:T(2,128)S(1)} %get-tuple-element.759) | copy-start | bytes 18436
  66.2 9.3 %collective-permute-start.6 = (f32[2,1,4,2,3,16,128]{6,5,1,3,0,4,2:T(8,128)S(1)}, f32[2,1,4,2,3,16,128]{6,5,1,3,0,4,2:T(8,128)S(1)}, u32[]{:S(2)}, u32[]{:S(2)}) collective-permute-start(f32[2,1,4,2,3,16,128]{6,5,1,3,0,4,2:T(8,128)S(1)} %get-tuple-element.235), channel_id=1, source_target_pairs={{0,8},{8,16},{16,24},{24,32},{32,40},{40,48},{48,56},{56,64},{64,7... | collective-permute-start | bytes 1179656 | tf_op jit(solution)/shard_map/ppermute | solution.py:29
  68.2 13.4 %collective-permute-start.7 = (f32[2,1,4,2,3,16,128]{6,5,1,3,0,4,2:T(8,128)S(1)}, f32[2,1,4,2,3,16,128]{6,5,1,3,0,4,2:T(8,128)S(1)}, u32[]{:S(2)}, u32[]{:S(2)}) collective-permute-start(f32[2,1,4,2,3,16,128]{6,5,1,3,0,4,2:T(8,128)S(1)} %get-tuple-element.236), channel_id=1, source_target_pairs={{8,0},{16,8},{24,16},{32,24},{40,32},{48,40},{56,48},{64,56},{72,6... | collective-permute-start | bytes 1179656 | tf_op jit(solution)/shard_map/ppermute | solution.py:31
  81.8 23.0 %collective-permute-start.8 = (f32[1,4,4,2,3,16,128]{6,5,1,3,0,4,2:T(8,128)S(1)}, f32[1,4,4,2,3,16,128]{6,5,1,3,0,4,2:T(8,128)S(1)}, u32[]{:S(2)}, u32[]{:S(2)}) collective-permute-start(f32[1,4,4,2,3,16,128]{6,5,1,3,0,4,2:T(8,128)S(1)} %get-tuple-element.185), channel_id=1, source_target_pairs={{0,1},{1,2},{2,3},{3,4},{4,5},{5,6},{6,7},{7,0},{8,9},{9,10},{10,1... | collective-permute-start | bytes 2359304 | tf_op jit(solution)/shard_map/ppermute | solution.py:29
  87.5 22.2 %collective-permute-start.9 = (f32[1,4,4,2,3,16,128]{6,5,1,3,0,4,2:T(8,128)S(1)}, f32[1,4,4,2,3,16,128]{6,5,1,3,0,4,2:T(8,128)S(1)}, u32[]{:S(2)}, u32[]{:S(2)}) collective-permute-start(f32[1,4,4,2,3,16,128]{6,5,1,3,0,4,2:T(8,128)S(1)} %get-tuple-element.186), channel_id=1, source_target_pairs={{1,0},{2,1},{3,2},{4,3},{5,4},{6,5},{7,6},{0,7},{9,8},{10,9},{11,1... | collective-permute-start | bytes 2359304 | tf_op jit(solution)/shard_map/ppermute | solution.py:31
  117.9 532.7 %copy-start = (bf16[2,2,256,256]{3,2,1,0:T(8,128)(2,1)S(1)}, bf16[2,2,256,256]{3,2,1,0:T(8,128)(2,1)}, u32[]{:S(2)}) copy-start(bf16[2,2,256,256]{3,2,1,0:T(8,128)(2,1)} %param.9) | copy-start | bytes 1572868
  652.6 14.7 %all-to-all-start = ((bf16[64,2,256,2]{2,1,3,0:T(2,128)(2,1)}), bf16[64,2,256,2]{2,1,3,0:T(2,128)(2,1)S(1)}, u32[]{:S(2)}, u32[]{:S(2)}) async-start(bf16[64,2,256,2]{2,1,3,0:T(2,128)(2,1)} %stack.619), calls=%async_computation | async-start | bytes 262144 | tf_op jit(solution)/shard_map/all_to_all | solution.py:234
  668.2 10.9 %collective-permute-start.10 = (f32[2,1,4,2,3,16,128]{6,5,1,3,0,4,2:T(8,128)S(1)}, f32[2,1,4,2,3,16,128]{6,5,1,3,0,4,2:T(8,128)S(1)}, u32[]{:S(2)}, u32[]{:S(2)}) collective-permute-start(f32[2,1,4,2,3,16,128]{6,5,1,3,0,4,2:T(8,128)S(1)} %get-tuple-element.223), channel_id=1, source_target_pairs={{0,8},{8,16},{16,24},{24,32},{32,40},{40,48},{48,56},{56,64},{64,7... | collective-permute-start | bytes 1179656 | tf_op jit(solution)/shard_map/ppermute | solution.py:29
  674.5 12.7 %collective-permute-start.11 = (f32[2,1,4,2,3,16,128]{6,5,1,3,0,4,2:T(8,128)S(1)}, f32[2,1,4,2,3,16,128]{6,5,1,3,0,4,2:T(8,128)S(1)}, u32[]{:S(2)}, u32[]{:S(2)}) collective-permute-start(f32[2,1,4,2,3,16,128]{6,5,1,3,0,4,2:T(8,128)S(1)} %get-tuple-element.224), channel_id=1, source_target_pairs={{8,0},{16,8},{24,16},{32,24},{40,32},{48,40},{56,48},{64,56},{72,6... | collective-permute-start | bytes 1179656 | tf_op jit(solution)/shard_map/ppermute | solution.py:31
  687.5 53.2 %collective-permute-start.12 = (f32[1,4,4,2,3,16,128]{6,5,1,3,0,4,2:T(8,128)S(1)}, f32[1,4,4,2,3,16,128]{6,5,1,3,0,4,2:T(8,128)S(1)}, u32[]{:S(2)}, u32[]{:S(2)}) collective-permute-start(f32[1,4,4,2,3,16,128]{6,5,1,3,0,4,2:T(8,128)S(1)} %get-tuple-element.180), channel_id=1, source_target_pairs={{0,1},{1,2},{2,3},{3,4},{4,5},{5,6},{6,7},{7,0},{8,9},{9,10},{10,1... | collective-permute-start | bytes 2359304 | tf_op jit(solution)/shard_map/ppermute | solution.py:29
  724.7 23.8 %collective-permute-start.13 = (f32[1,4,4,2,3,16,128]{6,5,1,3,0,4,2:T(8,128)S(1)}, f32[1,4,4,2,3,16,128]{6,5,1,3,0,4,2:T(8,128)S(1)}, u32[]{:S(2)}, u32[]{:S(2)}) collective-permute-start(f32[1,4,4,2,3,16,128]{6,5,1,3,0,4,2:T(8,128)S(1)} %get-tuple-element.181), channel_id=1, source_target_pairs={{1,0},{2,1},{3,2},{4,3},{5,4},{6,5},{7,6},{0,7},{9,8},{10,9},{11,1... | collective-permute-start | bytes 2359304 | tf_op jit(solution)/shard_map/ppermute | solution.py:31
  757.6 8.8 %collective-permute-start.14 = (f32[2,1,4,2,3,16,128]{6,5,1,3,2,0,4:T(8,128)S(1)}, f32[2,1,4,2,3,16,128]{6,5,1,3,2,0,4:T(8,128)S(1)}, u32[]{:S(2)}, u32[]{:S(2)}) collective-permute-start(f32[2,1,4,2,3,16,128]{6,5,1,3,2,0,4:T(8,128)S(1)} %get-tuple-element.211), channel_id=1, source_target_pairs={{0,8},{8,16},{16,24},{24,32},{32,40},{40,48},{48,56},{56,64},{64,7... | collective-permute-start | bytes 1179656 | tf_op jit(solution)/shard_map/ppermute | solution.py:29
  759.6 12.7 %collective-permute-start.15 = (f32[2,1,4,2,3,16,128]{6,5,1,3,2,0,4:T(8,128)S(1)}, f32[2,1,4,2,3,16,128]{6,5,1,3,2,0,4:T(8,128)S(1)}, u32[]{:S(2)}, u32[]{:S(2)}) collective-permute-start(f32[2,1,4,2,3,16,128]{6,5,1,3,2,0,4:T(8,128)S(1)} %get-tuple-element.212), channel_id=1, source_target_pairs={{8,0},{16,8},{24,16},{32,24},{40,32},{48,40},{56,48},{64,56},{72,6... | collective-permute-start | bytes 1179656 | tf_op jit(solution)/shard_map/ppermute | solution.py:31
  772.6 23.2 %collective-permute-start.16 = (f32[1,4,4,2,3,16,128]{6,5,1,3,2,0,4:T(8,128)S(1)}, f32[1,4,4,2,3,16,128]{6,5,1,3,2,0,4:T(8,128)S(1)}, u32[]{:S(2)}, u32[]{:S(2)}) collective-permute-start(f32[1,4,4,2,3,16,128]{6,5,1,3,2,0,4:T(8,128)S(1)} %get-tuple-element.178), channel_id=1, source_target_pairs={{0,1},{1,2},{2,3},{3,4},{4,5},{5,6},{6,7},{7,0},{8,9},{9,10},{10,1... | collective-permute-start | bytes 2359304 | tf_op jit(solution)/shard_map/ppermute | solution.py:29
  778.9 23.8 %collective-permute-start.17 = (f32[1,4,4,2,3,16,128]{6,5,1,3,2,0,4:T(8,128)S(1)}, f32[1,4,4,2,3,16,128]{6,5,1,3,2,0,4:T(8,128)S(1)}, u32[]{:S(2)}, u32[]{:S(2)}) collective-permute-start(f32[1,4,4,2,3,16,128]{6,5,1,3,2,0,4:T(8,128)S(1)} %get-tuple-element.179), channel_id=1, source_target_pairs={{1,0},{2,1},{3,2},{4,3},{5,4},{6,5},{7,6},{0,7},{9,8},{10,9},{11,1... | collective-permute-start | bytes 2359304 | tf_op jit(solution)/shard_map/ppermute | solution.py:31
  (49 other events, 924.5 us)
Sparse Core Ops, SparseCore 0:
  120.0 529.8 all-reduce.2
